TPU v7x, 128 devices: a whole 4x4x4 slice. The times are simulated.
128 devices in a mesh: attn: 4 (over x), expert: 32 (over y, z, core).
Axes of the slice: x: 4, y: 4, z: 4, core: 2. Of those that a mesh axis runs over, the one named last changes fastest.
Arguments:
- tokens: bfloat16 [2, 1024, 7168], P(None, ('attn', 'expert')), may hold values from -6 to 6
- routes: int32 [2, 1024, 8], P(None, ('attn', 'expert')), may hold values from 0 to 47, all different within a row; in each aligned block of 8 rows (0 to 7, 8 to 15, ..., all dimensions but the last counted through in order) at most 2 rows name the same one
- route_weights: float32 [2, 1024, 8], P(None, ('attn', 'expert')), may hold values from 0.2 to 1
- slot_expert: int32 [64], replicated, may hold values from 0 to 47, as said below
- w_gate: bfloat16 [64, 7168, 1024], P('expert', None, 'attn'), as said below
- w_up: bfloat16 [64, 7168, 1024], P('expert', None, 'attn'), as said below
- w_down: bfloat16 [64, 1024, 7168], P('expert', 'attn'), as said below
Outputs:
- combined: bfloat16 [2, 1024, 7168], P(None, ('attn', 'expert'))
Inputs may be any that keep to these rules, and one draw needn't show every extreme that they name: `routes`: in each micro-step at most 2 of one device's 8 rows choose the same expert, and some expert reaches 2. `slot_expert`: every expert of the window is held by at least one slot; some are held by several. `w_gate`: slots that hold the same expert hold identical gate projections. `w_up`: slots that hold the same expert hold identical up projections. `w_down`: slots that hold the same expert hold identical down projections.
All inputs are finite; a program needn't handle non-finite values.
Results may differ from a plain program's by a relative error of at most 0.0064.
Values may be sent and summed in bfloat16 or wider, within the bound.
No kernel may reach another device: no remote copies, remote signals or barrier semaphores. Data moves between devices by JAX's collectives and lax.ppermute only.
A program may use at most 128 MiB of HBM per device.

v0:
```python
import jax
import jax.numpy as jnp
from jax import lax
from jax.sharding import PartitionSpec as P

TOP = 8


def place_routes(chosen, slot_expert, replica_rank, slot_ids, earlier):
    matches = chosen[:, None] == slot_expert[None, :]
    replicas = jnp.sum(matches.astype(jnp.int32), axis=1)
    earlier_same = jnp.sum(
        ((chosen[:, None] == chosen[None, :]) & earlier).astype(jnp.int32), axis=1
    )
    replica_pick = earlier_same % replicas
    position = earlier_same // replicas
    selected = matches & (replica_rank[None, :] == replica_pick[:, None])
    target = jnp.sum(jnp.where(selected, slot_ids[None, :], 0), axis=1)
    return (target, position)


def run_quarter(row_block, gate_cols, up_cols, down_rows):
    gate_value = jnp.dot(row_block, gate_cols, preferred_element_type=jnp.float32)
    up_value = jnp.dot(row_block, up_cols, preferred_element_type=jnp.float32)
    hidden = (jax.nn.silu(gate_value) * up_value).astype(jnp.bfloat16)
    return jnp.dot(hidden, down_rows, preferred_element_type=jnp.float32)


def body(tokens, routes, route_weights, slot_expert, w_gate, w_up, w_down):
    groups = lax.axis_size("attn")
    columns = lax.axis_size("expert")
    holders = slot_expert.shape[0]
    per_device = holders // columns
    experts = 3 * holders // 4
    local_rows = tokens.shape[1]
    width = tokens.shape[2]
    capacity = max(2, (local_rows * TOP + experts - 1) // experts)
    route_total = local_rows * TOP
    cells = per_device * columns * capacity
    slot_ids = jnp.arange(holders, dtype=jnp.int32)
    same_holder = slot_expert[:, None] == slot_expert[None, :]
    replica_rank = jnp.sum(
        (same_holder & (slot_ids[None, :] < slot_ids[:, None])).astype(jnp.int32), axis=1
    )
    route_ids = jnp.arange(route_total, dtype=jnp.int32)
    earlier = route_ids[:, None] > route_ids[None, :]
    cell_ids = jnp.arange(cells, dtype=jnp.int32)
    outputs = []
    for micro in range(tokens.shape[0]):
        chosen = routes[micro].reshape(-1)
        token_rows = tokens[micro]
        target, position = place_routes(chosen, slot_expert, replica_rank, slot_ids, earlier)
        flat_cell = (target % per_device * columns + target // per_device) * capacity + position
        hits = (cell_ids[:, None] == flat_cell[None, :]).reshape(cells, local_rows, TOP)
        placing = jnp.any(hits, axis=2).astype(jnp.bfloat16)
        outgoing = jnp.dot(placing, token_rows, preferred_element_type=jnp.float32).astype(
            jnp.bfloat16
        )
        outgoing = outgoing.reshape(per_device, columns, capacity, width)
        copies = jnp.broadcast_to(outgoing[:, None], (per_device, groups, columns, capacity, width))
        copies = copies.reshape(per_device, groups * columns, capacity, width)
        arrived = lax.all_to_all(
            copies, ("attn", "expert"), split_axis=1, concat_axis=1, tiled=True
        )
        partials = []
        for slot_local in range(per_device):
            row_block = arrived[slot_local].reshape(-1, width)
            result = run_quarter(
                row_block, w_gate[slot_local], w_up[slot_local], w_down[slot_local]
            )
            partials.append(result.astype(jnp.bfloat16).reshape(groups, columns, capacity, width))
        partial_value = jnp.stack(partials, axis=0)
        pieces = partial_value.reshape(per_device, groups * columns, capacity, width)
        pieces = lax.all_to_all(pieces, ("attn", "expert"), split_axis=1, concat_axis=1, tiled=True)
        pieces = pieces.reshape(per_device, groups, columns, capacity, width)
        returned = jnp.sum(pieces.astype(jnp.float32), axis=1).astype(jnp.bfloat16)
        returned = returned.reshape(cells, width)
        picked = returned[flat_cell].astype(jnp.float32)
        weights_now = route_weights[micro].reshape(-1)
        blended = jnp.sum((picked * weights_now[:, None]).reshape(local_rows, TOP, width), axis=1)
        outputs.append(blended.astype(jnp.bfloat16))
    return jnp.stack(outputs)


def solution(mesh):
    in_specs = (
        P(None, ("attn", "expert"), None),
        P(None, ("attn", "expert"), None),
        P(None, ("attn", "expert"), None),
        P(),
        P("expert", None, "attn"),
        P("expert", None, "attn"),
        P("expert", "attn", None),
    )
    out_specs = P(None, ("attn", "expert"), None)
    return jax.shard_map(body, mesh=mesh, in_specs=in_specs, out_specs=out_specs, check_vma=False)
```

profile of v0, /device:TPU:23, one launch (start us, length us, event | category | flops | bytes accessed | tf_op | source)
XLA Modules:
  0.0 447.9 jit_solution(13728672464697637354)
XLA Ops:
  15.6 11.0 %all-to-all-start = ((bf16[2,128,2,7168]{3,2,0,1:T(2,128)(2,1)}), bf16[2,128,2,7168]{3,2,0,1:T(2,128)(2,1)}, u32[]{:S(2)}, u32[]{:S(2)}) async-start(bf16[2,128,2,7168]{3,2,0,1:T(2,128)(2,1)} %bitcast.160), calls=%async_computation | async-start | bytes 14680064 | tf_op jit(solution)/shard_map/all_to_all | solution.py:62
  32.2 86.8 %all-to-all-done = bf16[2,128,2,7168]{3,2,0,1:T(2,128)(2,1)} async-done(((bf16[2,128,2,7168]{3,2,0,1:T(2,128)(2,1)}), bf16[2,128,2,7168]{3,2,0,1:T(2,128)(2,1)}, u32[]{:S(2)}, u32[]{:S(2)}) %all-to-all-start) | async-done | bytes 7340064 | tf_op jit(solution)/shard_map/all_to_all | solution.py:62
  132.7 7.7 %fusion.129 = (bf16[1,128,2,7168]{3,2,0,1:T(2,128)(2,1)}, bf16[1,128,2,7168]{3,2,0,1:T(2,128)(2,1)}) fusion(bf16[2,128,2,7168]{3,2,0,1:T(2,128)(2,1)} %all-to-all-done), kind=kLoop, calls=%fused_computation.173 | loop fusion | bytes 14680064 | tf_op jit(solution)/shard_map/slice | solution.py:67
  140.4 8.4 %reshape_squeeze.12 = bf16[256,7168]{1,0:T(8,128)(2,1)} reshape(bf16[1,128,2,7168]{3,2,0,1:T(2,128)(2,1)} %get-tuple-element.18) | data formatting | bytes 7340032 | tf_op jit(solution)/shard_map/reshape;squeeze | solution.py:67
  153.1 10.1 %convolution_convert_fusion.3 = bf16[256,7168]{1,0:T(8,128)(2,1)} fusion(bf16[2,256,7168]{2,1,0:T(8,128)(2,1)} %param.13, bf16[256,7168]{1,0:T(8,128)(2,1)} %reshape_squeeze.12, bf16[2,7168,256]{2,1,0:T(8,128)(2,1)} %param.12, f32[256,256]{1,0:T(8,128)S(1)} %fusion.18), kind=kOutput, calls=%fused_computation.5 | convolution fusion | flops 1881276416 | bytes 14942208 | tf_op jit(solution)/shard_map/dot_general | solution.py:26
  163.2 8.1 %stack.19 = bf16[1,128,2,7168]{3,2,1,0:T(2,128)(2,1)} reshape(bf16[256,7168]{1,0:T(8,128)(2,1)} %convolution_convert_fusion.3) | data formatting | bytes 7340032 | tf_op jit(solution)/shard_map/stack | solution.py:72
  171.3 8.6 %reshape_squeeze.13 = bf16[256,7168]{1,0:T(8,128)(2,1)} reshape(bf16[1,128,2,7168]{3,2,0,1:T(2,128)(2,1)} %get-tuple-element.19) | data formatting | bytes 7340032 | tf_op jit(solution)/shard_map/reshape;squeeze | solution.py:67
  184.2 10.1 %convolution_convert_fusion.2 = bf16[256,7168]{1,0:T(8,128)(2,1)} fusion(bf16[2,256,7168]{2,1,0:T(8,128)(2,1)} %param.13, bf16[256,7168]{1,0:T(8,128)(2,1)} %reshape_squeeze.13, bf16[2,7168,256]{2,1,0:T(8,128)(2,1)} %param.12, f32[256,256]{1,0:T(8,128)S(1)} %fusion.8), kind=kOutput, calls=%fused_computation.4 | convolution fusion | flops 1881276416 | bytes 14942208 | tf_op jit(solution)/shard_map/dot_general | solution.py:26
  194.3 8.1 %stack.20 = bf16[1,128,2,7168]{3,2,1,0:T(2,128)(2,1)} reshape(bf16[256,7168]{1,0:T(8,128)(2,1)} %convolution_convert_fusion.2) | data formatting | bytes 7340032 | tf_op jit(solution)/shard_map/stack | solution.py:72
  202.4 11.8 %pad_maximum_fusion = bf16[2,128,2,7168]{3,2,0,1:T(2,128)(2,1)} fusion(bf16[1,128,2,7168]{3,2,0,1:T(2,128)(2,1)} %bitcast.164, bf16[1,128,2,7168]{3,2,0,1:T(2,128)(2,1)} %bitcast.162), kind=kLoop, calls=%fused_computation.8 | loop fusion | flops 3670016 | bytes 14680064 | tf_op jit(solution)/shard_map/stack | solution.py:72
  214.2 9.1 %all-to-all-done.2 = bf16[2,128,2,7168]{3,2,0,1:T(2,128)(2,1)} async-done(((bf16[2,128,2,7168]{3,2,0,1:T(2,128)(2,1)}), bf16[2,128,2,7168]{3,2,0,1:T(2,128)(2,1)}, u32[]{:S(2)}, u32[]{:S(2)}) %all-to-all-start.2) | async-done | bytes 7340064 | tf_op jit(solution)/shard_map/all_to_all | solution.py:62
  223.4 7.7 %all-to-all-start.1 = ((bf16[2,128,2,7168]{3,2,0,1:T(2,128)(2,1)}), bf16[2,128,2,7168]{3,2,0,1:T(2,128)(2,1)}, u32[]{:S(2)}, u32[]{:S(2)}) async-start(bf16[2,128,2,7168]{3,2,0,1:T(2,128)(2,1)} %pad_maximum_fusion), calls=%async_computation.1 | async-start | bytes 14680064 | tf_op jit(solution)/shard_map/all_to_all | solution.py:74
  231.1 7.7 %fusion.130 = (bf16[1,128,2,7168]{3,2,0,1:T(2,128)(2,1)}, bf16[1,128,2,7168]{3,2,0,1:T(2,128)(2,1)}) fusion(bf16[2,128,2,7168]{3,2,0,1:T(2,128)(2,1)} %all-to-all-done.2), kind=kLoop, calls=%fused_computation.174 | loop fusion | bytes 14680064 | tf_op jit(solution)/shard_map/slice | solution.py:67
  238.8 8.4 %reshape_squeeze.14 = bf16[256,7168]{1,0:T(8,128)(2,1)} reshape(bf16[1,128,2,7168]{3,2,0,1:T(2,128)(2,1)} %get-tuple-element.20) | data formatting | bytes 7340032 | tf_op jit(solution)/shard_map/reshape;squeeze | solution.py:67
  251.5 10.0 %convolution_convert_fusion.1 = bf16[256,7168]{1,0:T(8,128)(2,1)} fusion(bf16[2,256,7168]{2,1,0:T(8,128)(2,1)} %param.13, bf16[256,7168]{1,0:T(8,128)(2,1)} %reshape_squeeze.14, bf16[2,7168,256]{2,1,0:T(8,128)(2,1)} %param.12, f32[256,256]{1,0:T(8,128)S(1)} %fusion.16), kind=kOutput, calls=%fused_computation.3 | convolution fusion | flops 1881276416 | bytes 14942208 | tf_op jit(solution)/shard_map/dot_general | solution.py:26
  261.5 8.1 %stack.22 = bf16[1,128,2,7168]{3,2,1,0:T(2,128)(2,1)} reshape(bf16[256,7168]{1,0:T(8,128)(2,1)} %convolution_convert_fusion.1) | data formatting | bytes 7340032 | tf_op jit(solution)/shard_map/stack | solution.py:72
  269.7 8.8 %reshape_squeeze.15 = bf16[256,7168]{1,0:T(8,128)(2,1)} reshape(bf16[1,128,2,7168]{3,2,0,1:T(2,128)(2,1)} %get-tuple-element.21) | data formatting | bytes 7340032 | tf_op jit(solution)/shard_map/reshape;squeeze | solution.py:67
  282.8 10.0 %convolution_convert_fusion = bf16[256,7168]{1,0:T(8,128)(2,1)} fusion(bf16[2,256,7168]{2,1,0:T(8,128)(2,1)} %param.13, bf16[256,7168]{1,0:T(8,128)(2,1)} %reshape_squeeze.15, bf16[2,7168,256]{2,1,0:T(8,128)(2,1)} %param.12, f32[256,256]{1,0:T(8,128)S(1)} %fusion.6), kind=kOutput, calls=%fused_computation.2 | convolution fusion | flops 1881276416 | bytes 14942208 | tf_op jit(solution)/shard_map/dot_general | solution.py:26
  292.8 8.1 %stack.23 = bf16[1,128,2,7168]{3,2,1,0:T(2,128)(2,1)} reshape(bf16[256,7168]{1,0:T(8,128)(2,1)} %convolution_convert_fusion) | data formatting | bytes 7340032 | tf_op jit(solution)/shard_map/stack | solution.py:72
  300.9 11.8 %pad_maximum_fusion.1 = bf16[2,128,2,7168]{3,2,0,1:T(2,128)(2,1)} fusion(bf16[1,128,2,7168]{3,2,0,1:T(2,128)(2,1)} %bitcast.165, bf16[1,128,2,7168]{3,2,0,1:T(2,128)(2,1)} %bitcast.163), kind=kLoop, calls=%fused_computation.9 | loop fusion | flops 3670016 | bytes 14680064 | tf_op jit(solution)/shard_map/stack | solution.py:72
  312.7 9.0 %all-to-all-done.1 = bf16[2,128,2,7168]{3,2,0,1:T(2,128)(2,1)} async-done(((bf16[2,128,2,7168]{3,2,0,1:T(2,128)(2,1)}), bf16[2,128,2,7168]{3,2,0,1:T(2,128)(2,1)}, u32[]{:S(2)}, u32[]{:S(2)}) %all-to-all-start.1) | async-done | bytes 7340064 | tf_op jit(solution)/shard_map/all_to_all | solution.py:74
  329.5 10.2 %reduce_sum.118 = bf16[2,32,2,7168]{3,2,0,1:T(2,128)(2,1)S(1)} reduce(bf16[2,4,32,2,7168]{4,3,0,2,1:T(2,128)(2,1)} %bitcast.10, bf16[]{:T(256)} %constant.73.clone.1), dimensions={1}, to_apply=%region_5.6 | reduce | flops 2752512 | bytes 9175042 | tf_op jit(solution)/shard_map/reduce_sum | solution.py:76
  346.2 73.9 %all-to-all-done.3 = bf16[2,128,2,7168]{3,2,0,1:T(2,128)(2,1)} async-done(((bf16[2,128,2,7168]{3,2,0,1:T(2,128)(2,1)}), bf16[2,128,2,7168]{3,2,0,1:T(2,128)(2,1)}, u32[]{:S(2)}, u32[]{:S(2)}) %all-to-all-start.3) | async-done | bytes 7340064 | tf_op jit(solution)/shard_map/all_to_all | solution.py:74
  420.0 11.4 %reduce_sum.125 = bf16[2,32,2,7168]{3,2,0,1:T(2,128)(2,1)} reduce(bf16[2,4,32,2,7168]{4,3,0,2,1:T(2,128)(2,1)} %bitcast.22, bf16[]{:T(256)} %constant.73.clone.1), dimensions={1}, to_apply=%region_11.12 | reduce | flops 2752512 | bytes 9175042 | tf_op jit(solution)/shard_map/reduce_sum | solution.py:76
  (48 shorter events, 82.3 us)
Async XLA Ops:
  15.6 11.5 %copy-start = (bf16[2,8,7168]{2,1,0:T(8,128)(2,1)S(1)}, bf16[2,8,7168]{2,1,0:T(8,128)(2,1)}, u32[]{:S(2)}) copy-start(bf16[2,8,7168]{2,1,0:T(8,128)(2,1)} %param.7) | copy-start | bytes 688132
  15.6 103.4 %all-to-all-start = ((bf16[2,128,2,7168]{3,2,0,1:T(2,128)(2,1)}), bf16[2,128,2,7168]{3,2,0,1:T(2,128)(2,1)}, u32[]{:S(2)}, u32[]{:S(2)}) async-start(bf16[2,128,2,7168]{3,2,0,1:T(2,128)(2,1)} %bitcast.160), calls=%async_computation | async-start | bytes 14680064 | tf_op jit(solution)/shard_map/all_to_all | solution.py:62
  125.1 98.3 %all-to-all-start.2 = ((bf16[2,128,2,7168]{3,2,0,1:T(2,128)(2,1)}), bf16[2,128,2,7168]{3,2,0,1:T(2,128)(2,1)}, u32[]{:S(2)}, u32[]{:S(2)}) async-start(bf16[2,128,2,7168]{3,2,0,1:T(2,128)(2,1)} %bitcast.161), calls=%async_computation.2 | async-start | bytes 14680064 | tf_op jit(solution)/shard_map/all_to_all | solution.py:62
  223.4 98.4 %all-to-all-start.1 = ((bf16[2,128,2,7168]{3,2,0,1:T(2,128)(2,1)}), bf16[2,128,2,7168]{3,2,0,1:T(2,128)(2,1)}, u32[]{:S(2)}, u32[]{:S(2)}) async-start(bf16[2,128,2,7168]{3,2,0,1:T(2,128)(2,1)} %pad_maximum_fusion), calls=%async_computation.1 | async-start | bytes 14680064 | tf_op jit(solution)/shard_map/all_to_all | solution.py:74
  312.7 16.7 %copy-start.1 = (f32[2,8,8]{2,1,0:T(8,128)S(1)}, f32[2,8,8]{2,1,0:T(8,128)}, u32[]{:S(2)}) copy-start(f32[2,8,8]{2,1,0:T(8,128)} %param.9) | copy-start | bytes 1540
  321.7 98.3 %all-to-all-start.3 = ((bf16[2,128,2,7168]{3,2,0,1:T(2,128)(2,1)}), bf16[2,128,2,7168]{3,2,0,1:T(2,128)(2,1)}, u32[]{:S(2)}, u32[]{:S(2)}) async-start(bf16[2,128,2,7168]{3,2,0,1:T(2,128)(2,1)} %pad_maximum_fusion.1), calls=%async_computation.3 | async-start | bytes 14680064 | tf_op jit(solution)/shard_map/all_to_all | solution.py:74
where the time goes:
time: 455 us; the launch traced here: 448 us
  waiting for transfers between devices  179 us (39%)
  local copies, waits for them, and re-layouts  125 us (27%)
  matrix products  59.6 us (13%)
  other arithmetic  49.9 us (11%)
  starting transfers between devices  34 us (7%)
    all_to_all x2, waiting for transfers between devices, body(): lax.all_to_all(copies, ('attn', 'expert'), split_axis=1, concat_axis=1, t...  96 us
    all_to_all x2, waiting for transfers between devices, body(): lax.all_to_all(pieces, ('attn', 'expert'), split_axis=1, concat_axis=1, t...  82.9 us
    dot_general x4, matrix products, run_quarter(): return jnp.dot(hidden, down_rows, preferred_element_type=jnp.float32)  40.3 us
    another operation x4, local copies, waits for them, and re-layouts, body(): row_block = arrived[slot_local].reshape(-1, width)  34.2 us
    another operation x4, local copies, waits for them, and re-layouts, body(): partial_value = jnp.stack(partials, axis=0)  32.5 us
    another operation x2, other arithmetic, body(): partial_value = jnp.stack(partials, axis=0)  23.6 us
    reduce_sum x2, other arithmetic, body(): returned = jnp.sum(pieces.astype(jnp.float32), axis=1).astype(jnp.bfloat16)  21.6 us
    broadcast_in_dim x6, local copies, waits for them, and re-layouts, body(): jnp.broadcast_to(outgoing[:, None], (per_device, groups, columns, capacit...  21.1 us
  transfers between devices with their start and end apart: 4, of which 4 were waited for; matrix products, arithmetic and copies ran while one was open for 41% of the time, Pallas kernels for 0%

commit v1 on v0

--- a/solution.py
+++ b/solution.py
@@ -71,7 +71,11 @@
             partials.append(result.astype(jnp.bfloat16).reshape(groups, columns, capacity, width))
         partial_value = jnp.stack(partials, axis=0)
         pieces = partial_value.reshape(per_device, groups * columns, capacity, width)
-        pieces = lax.all_to_all(pieces, ("attn", "expert"), split_axis=1, concat_axis=1, tiled=True)
+        m_next = lax.psum(1, axis_name=("attn", "expert"))
+        arr_out = jnp.split(pieces, m_next, axis=1)
+        z1 = jnp.stack(arr_out, axis=0)
+        block_out = lax.all_to_all(z1, concat_axis=0, axis_name=("attn", "expert"), split_axis=0)
+        pieces = jnp.concatenate(block_out, axis=1)
         pieces = pieces.reshape(per_device, groups, columns, capacity, width)
         returned = jnp.sum(pieces.astype(jnp.float32), axis=1).astype(jnp.bfloat16)
         returned = returned.reshape(cells, width)

time: 455 us -> 722 us (1.59); the launches traced: 448 us -> 707 us
  local copies, waits for them, and re-layouts: 125 us -> 419 us
  other arithmetic: 49.9 us -> 26.4 us
  waiting for transfers between devices: 179 us -> 162 us
    unnamed x4 -> x262, local copies, waits for them, and re-layouts: 0.01 us -> 282 us
    another operation x2 -> x0, other arithmetic: 23.6 us -> none  [body(): partial_value = jnp.stack(partials, axis=0)]
    another operation x4 -> x6, local copies, waits for them, and re-layouts: 32.5 us -> 41.8 us  [body(): partial_value = jnp.stack(partials, axis=0)]
    all_to_all x2, waiting for transfers between devices: 96 us -> 86.8 us  [body(): lax.all_to_all(copies, ('attn', 'expert'), split_axis=1, concat_axis=1, t...]
    all_to_all x2, waiting for transfers between devices: 82.9 us -> 75.6 us  [body(): lax.all_to_all(z1, concat_axis=0, axis_name=('attn', 'expert'), split_axi...]
  transfers between devices with their start and end apart: 4 -> 4, of which waited for: 4 -> 2; matrix products, arithmetic and copies ran while one was open for 41% -> 64% of each run, Pallas kernels for 0% -> 0%
where the time goes in v1:
time: 722 us; the launch traced here: 707 us
  local copies, waits for them, and re-layouts  419 us (58%)
  waiting for transfers between devices  162 us (22%)
  matrix products  59.5 us (8%)
  starting transfers between devices  39.9 us (6%)
  other arithmetic  26.4 us (4%)
    unnamed x262, local copies, waits for them, and re-layouts  282 us
    all_to_all x2, waiting for transfers between devices, body(): lax.all_to_all(copies, ('attn', 'expert'), split_axis=1, concat_axis=1, t...  86.8 us
    all_to_all x2, waiting for transfers between devices, body(): lax.all_to_all(z1, concat_axis=0, axis_name=('attn', 'expert'), split_axi...  75.6 us
    another operation x6, local copies, waits for them, and re-layouts, body(): partial_value = jnp.stack(partials, axis=0)  41.8 us
    dot_general x4, matrix products, run_quarter(): return jnp.dot(hidden, down_rows, preferred_element_type=jnp.float32)  40.1 us
    another operation x4, local copies, waits for them, and re-layouts, body(): row_block = arrived[slot_local].reshape(-1, width)  33.8 us
    reduce_sum x2, other arithmetic, body(): returned = jnp.sum(pieces.astype(jnp.float32), axis=1).astype(jnp.bfloat16)  21.6 us
    broadcast_in_dim x6, local copies, waits for them, and re-layouts, body(): jnp.broadcast_to(outgoing[:, None], (per_device, groups, columns, capacit...  21.1 us
  transfers between devices with their start and end apart: 4, of which 2 were waited for; matrix products, arithmetic and copies ran while one was open for 64% of the time, Pallas kernels for 0%

profile of v1, /device:TPU:23, one launch (start us, length us, event | category | flops | bytes accessed | tf_op | source)
XLA Modules:
  0.0 707.5 jit_solution(4725369940107437729)
XLA Ops:
  15.6 11.0 %all-to-all-start = ((bf16[2,128,2,7168]{3,2,0,1:T(2,128)(2,1)}), bf16[2,128,2,7168]{3,2,0,1:T(2,128)(2,1)}, u32[]{:S(2)}, u32[]{:S(2)}) async-start(bf16[2,128,2,7168]{3,2,0,1:T(2,128)(2,1)} %bitcast.1693), calls=%async_computation | async-start | bytes 14680064 | tf_op jit(solution)/shard_map/all_to_all | solution.py:62
  32.2 86.8 %all-to-all-done = bf16[2,128,2,7168]{3,2,0,1:T(2,128)(2,1)} async-done(((bf16[2,128,2,7168]{3,2,0,1:T(2,128)(2,1)}), bf16[2,128,2,7168]{3,2,0,1:T(2,128)(2,1)}, u32[]{:S(2)}, u32[]{:S(2)}) %all-to-all-start) | async-done | bytes 7340064 | tf_op jit(solution)/shard_map/all_to_all | solution.py:62
  125.1 8.0 %all-to-all-start.2 = ((bf16[2,128,2,7168]{3,2,0,1:T(2,128)(2,1)}), bf16[2,128,2,7168]{3,2,0,1:T(2,128)(2,1)}, u32[]{:S(2)}, u32[]{:S(2)}) async-start(bf16[2,128,2,7168]{3,2,0,1:T(2,128)(2,1)} %bitcast.1692), calls=%async_computation.2 | async-start | bytes 14680064 | tf_op jit(solution)/shard_map/all_to_all | solution.py:62
  133.1 7.7 %fusion.129 = (bf16[1,128,2,7168]{3,2,0,1:T(2,128)(2,1)}, bf16[1,128,2,7168]{3,2,0,1:T(2,128)(2,1)}) fusion(bf16[2,128,2,7168]{3,2,0,1:T(2,128)(2,1)} %all-to-all-done), kind=kLoop, calls=%fused_computation.687 | loop fusion | bytes 14680064 | tf_op jit(solution)/shard_map/slice | solution.py:67
  140.8 8.4 %reshape_squeeze.12 = bf16[256,7168]{1,0:T(8,128)(2,1)} reshape(bf16[1,128,2,7168]{3,2,0,1:T(2,128)(2,1)} %get-tuple-element.19) | data formatting | bytes 7340032 | tf_op jit(solution)/shard_map/reshape;squeeze | solution.py:67
  153.5 10.1 %convolution_convert_fusion.3 = bf16[256,7168]{1,0:T(8,128)(2,1)} fusion(bf16[2,256,7168]{2,1,0:T(8,128)(2,1)} %param.13, bf16[256,7168]{1,0:T(8,128)(2,1)} %reshape_squeeze.12, bf16[2,7168,256]{2,1,0:T(8,128)(2,1)} %param.12, f32[256,256]{1,0:T(8,128)S(1)} %fusion.18), kind=kOutput, calls=%fused_computation.5 | convolution fusion | flops 1881276416 | bytes 14942208 | tf_op jit(solution)/shard_map/dot_general | solution.py:26
  163.5 8.1 %stack.793 = bf16[1,128,2,7168]{3,2,1,0:T(2,128)(2,1)} reshape(bf16[256,7168]{1,0:T(8,128)(2,1)} %convolution_convert_fusion.3) | data formatting | bytes 7340032 | tf_op jit(solution)/shard_map/stack | solution.py:72
  171.7 6.3 constant_dynamic-update-slice_fusion.1
  178.0 8.6 %reshape_squeeze.13 = bf16[256,7168]{1,0:T(8,128)(2,1)} reshape(bf16[1,128,2,7168]{3,2,0,1:T(2,128)(2,1)} %get-tuple-element.18) | data formatting | bytes 7340032 | tf_op jit(solution)/shard_map/reshape;squeeze | solution.py:67
  190.8 10.0 %convolution_convert_fusion.2 = bf16[256,7168]{1,0:T(8,128)(2,1)} fusion(bf16[2,256,7168]{2,1,0:T(8,128)(2,1)} %param.13, bf16[256,7168]{1,0:T(8,128)(2,1)} %reshape_squeeze.13, bf16[2,7168,256]{2,1,0:T(8,128)(2,1)} %param.12, f32[256,256]{1,0:T(8,128)S(1)} %fusion.8), kind=kOutput, calls=%fused_computation.4 | convolution fusion | flops 1881276416 | bytes 14942208 | tf_op jit(solution)/shard_map/dot_general | solution.py:26
  200.9 8.1 %stack.794 = bf16[1,128,2,7168]{3,2,1,0:T(2,128)(2,1)} reshape(bf16[256,7168]{1,0:T(8,128)(2,1)} %convolution_convert_fusion.2) | data formatting | bytes 7340032 | tf_op jit(solution)/shard_map/stack | solution.py:72
  209.0 6.4 constant_dynamic-update-slice_fusion
  404.6 10.7 %all-to-all-start.1 = ((bf16[128,2,1,2,7168]{4,3,1,2,0:T(2,128)(2,1)}), bf16[128,2,1,2,7168]{4,3,1,2,0:T(2,128)(2,1)}, u32[]{:S(2)}, u32[]{:S(2)}) async-start(bf16[128,2,1,2,7168]{4,3,1,2,0:T(2,128)(2,1)} %constant_dynamic-update-slice_fusion.2), calls=%async_computation.1 | async-start | bytes 14680064 | tf_op jit(solution)/shard_map/all_to_all | solution.py:77
  415.3 7.7 %fusion.130 = (bf16[1,128,2,7168]{3,2,0,1:T(2,128)(2,1)}, bf16[1,128,2,7168]{3,2,0,1:T(2,128)(2,1)}) fusion(bf16[2,128,2,7168]{3,2,0,1:T(2,128)(2,1)} %all-to-all-done.2), kind=kLoop, calls=%fused_computation.688 | loop fusion | bytes 14680064 | tf_op jit(solution)/shard_map/slice | solution.py:67
  423.1 8.4 %reshape_squeeze.15 = bf16[256,7168]{1,0:T(8,128)(2,1)} reshape(bf16[1,128,2,7168]{3,2,0,1:T(2,128)(2,1)} %get-tuple-element.20) | data formatting | bytes 7340032 | tf_op jit(solution)/shard_map/reshape;squeeze | solution.py:67
  435.7 10.0 %convolution_convert_fusion = bf16[256,7168]{1,0:T(8,128)(2,1)} fusion(bf16[2,256,7168]{2,1,0:T(8,128)(2,1)} %param.13, bf16[256,7168]{1,0:T(8,128)(2,1)} %reshape_squeeze.15, bf16[2,7168,256]{2,1,0:T(8,128)(2,1)} %param.12, f32[256,256]{1,0:T(8,128)S(1)} %fusion.6), kind=kOutput, calls=%fused_computation.2 | convolution fusion | flops 1881276416 | bytes 14942208 | tf_op jit(solution)/shard_map/dot_general | solution.py:26
  445.8 8.1 %stack.926 = bf16[1,128,2,7168]{3,2,1,0:T(2,128)(2,1)} reshape(bf16[256,7168]{1,0:T(8,128)(2,1)} %convolution_convert_fusion) | data formatting | bytes 7340032 | tf_op jit(solution)/shard_map/stack | solution.py:72
  453.9 8.4 %reshape_squeeze.14 = bf16[256,7168]{1,0:T(8,128)(2,1)} reshape(bf16[1,128,2,7168]{3,2,0,1:T(2,128)(2,1)} %get-tuple-element.21) | data formatting | bytes 7340032 | tf_op jit(solution)/shard_map/reshape;squeeze | solution.py:67
  466.6 10.0 %convolution_convert_fusion.1 = bf16[256,7168]{1,0:T(8,128)(2,1)} fusion(bf16[2,256,7168]{2,1,0:T(8,128)(2,1)} %param.13, bf16[256,7168]{1,0:T(8,128)(2,1)} %reshape_squeeze.14, bf16[2,7168,256]{2,1,0:T(8,128)(2,1)} %param.12, f32[256,256]{1,0:T(8,128)S(1)} %fusion.16), kind=kOutput, calls=%fused_computation.3 | convolution fusion | flops 1881276416 | bytes 14942208 | tf_op jit(solution)/shard_map/dot_general | solution.py:26
  476.6 8.3 %stack.925 = bf16[1,128,2,7168]{3,2,1,0:T(2,128)(2,1)} reshape(bf16[256,7168]{1,0:T(8,128)(2,1)} %convolution_convert_fusion.1) | data formatting | bytes 7340032 | tf_op jit(solution)/shard_map/stack | solution.py:72
  576.9 10.2 %all-to-all-start.3 = ((bf16[128,2,1,2,7168]{4,3,1,2,0:T(2,128)(2,1)}), bf16[128,2,1,2,7168]{4,3,1,2,0:T(2,128)(2,1)}, u32[]{:S(2)}, u32[]{:S(2)}) async-start(bf16[128,2,1,2,7168]{4,3,1,2,0:T(2,128)(2,1)} %constant_dynamic-update-slice_fusion.132), calls=%async_computation.3 | async-start | bytes 14680064 | tf_op jit(solution)/shard_map/all_to_all | solution.py:77
  587.1 10.2 %reduce_sum.118 = bf16[2,32,2,7168]{3,2,0,1:T(2,128)(2,1)S(1)} reduce(bf16[2,4,32,2,7168]{4,3,0,2,1:T(2,128)(2,1)} %bitcast.137, bf16[]{:T(256)} %constant.73.clone.1), dimensions={1}, to_apply=%region_5.6 | reduce | flops 2752512 | bytes 9175042 | tf_op jit(solution)/shard_map/reduce_sum | solution.py:80
  603.9 75.6 %all-to-all-done.3 = bf16[128,2,1,2,7168]{4,3,1,2,0:T(2,128)(2,1)} async-done(((bf16[128,2,1,2,7168]{4,3,1,2,0:T(2,128)(2,1)}), bf16[128,2,1,2,7168]{4,3,1,2,0:T(2,128)(2,1)}, u32[]{:S(2)}, u32[]{:S(2)}) %all-to-all-start.3) | async-done | bytes 7340064 | tf_op jit(solution)/shard_map/all_to_all | solution.py:77
  679.5 11.5 %reduce_sum.125 = bf16[2,32,2,7168]{3,2,0,1:T(2,128)(2,1)} reduce(bf16[2,4,32,2,7168]{4,3,0,2,1:T(2,128)(2,1)} %bitcast.276, bf16[]{:T(256)} %constant.73.clone.1), dimensions={1}, to_apply=%region_11.12 | reduce | flops 2752512 | bytes 9175042 | tf_op jit(solution)/shard_map/reduce_sum | solution.py:80
  (308 shorter events, 348.2 us)
Async XLA Ops:
  15.6 11.5 %copy-start.1 = (bf16[2,8,7168]{2,1,0:T(8,128)(2,1)S(1)}, bf16[2,8,7168]{2,1,0:T(8,128)(2,1)}, u32[]{:S(2)}) copy-start(bf16[2,8,7168]{2,1,0:T(8,128)(2,1)} %param.7) | copy-start | bytes 688132
  15.6 103.4 %all-to-all-start = ((bf16[2,128,2,7168]{3,2,0,1:T(2,128)(2,1)}), bf16[2,128,2,7168]{3,2,0,1:T(2,128)(2,1)}, u32[]{:S(2)}, u32[]{:S(2)}) async-start(bf16[2,128,2,7168]{3,2,0,1:T(2,128)(2,1)} %bitcast.1693), calls=%async_computation | async-start | bytes 14680064 | tf_op jit(solution)/shard_map/all_to_all | solution.py:62
  125.1 279.5 %all-to-all-start.2 = ((bf16[2,128,2,7168]{3,2,0,1:T(2,128)(2,1)}), bf16[2,128,2,7168]{3,2,0,1:T(2,128)(2,1)}, u32[]{:S(2)}, u32[]{:S(2)}) async-start(bf16[2,128,2,7168]{3,2,0,1:T(2,128)(2,1)} %bitcast.1692), calls=%async_computation.2 | async-start | bytes 14680064 | tf_op jit(solution)/shard_map/all_to_all | solution.py:62
  404.6 172.3 %all-to-all-start.1 = ((bf16[128,2,1,2,7168]{4,3,1,2,0:T(2,128)(2,1)}), bf16[128,2,1,2,7168]{4,3,1,2,0:T(2,128)(2,1)}, u32[]{:S(2)}, u32[]{:S(2)}) async-start(bf16[128,2,1,2,7168]{4,3,1,2,0:T(2,128)(2,1)} %constant_dynamic-update-slice_fusion.2), calls=%async_computation.1 | async-start | bytes 14680064 | tf_op jit(solution)/shard_map/all_to_all | solution.py:77
  484.9 4.7 copy-start
  576.9 10.2 %copy-start.2 = (f32[2,8,8]{2,1,0:T(8,128)S(1)}, f32[2,8,8]{2,1,0:T(8,128)}, u32[]{:S(2)}) copy-start(f32[2,8,8]{2,1,0:T(8,128)} %param.9) | copy-start | bytes 1540
  576.9 102.6 %all-to-all-start.3 = ((bf16[128,2,1,2,7168]{4,3,1,2,0:T(2,128)(2,1)}), bf16[128,2,1,2,7168]{4,3,1,2,0:T(2,128)(2,1)}, u32[]{:S(2)}, u32[]{:S(2)}) async-start(bf16[128,2,1,2,7168]{4,3,1,2,0:T(2,128)(2,1)} %constant_dynamic-update-slice_fusion.132), calls=%async_computation.3 | async-start | bytes 14680064 | tf_op jit(solution)/shard_map/all_to_all | solution.py:77
